TPU v7x, 32 devices: a whole 2x2x4 slice. The times are simulated.
32 devices in a mesh: groups: 1, seq: 32 (over z, y, x, core).
Axes of the slice: x: 2, y: 2, z: 4, core: 2. Of those that a mesh axis runs over, the one named last changes fastest.
Arguments:
- features: bfloat16 [2, 4096, 1536], P('groups', 'seq'), may hold values from -6 to 6
- cotangent: bfloat16 [2, 4096, 1536], P('groups', 'seq'), may hold values from -6 to 6
- dilated_kernel_weight: bfloat16 [1536, 3, 768], P('seq'), may hold values from -0.09375 to 0.09375
- project_weight: bfloat16 [1536, 768], P('seq'), may hold values from -0.21875 to 0.21875
- outer_gain: float32 [1536], replicated, may hold values from 0.1 to 1.9
- inner_gain: float32 [768], replicated, may hold values from 0.1 to 1.9
Outputs:
- block_out: bfloat16 [2, 4096, 1536], P('groups', 'seq')
- grad_features: bfloat16 [2, 4096, 1536], P('groups', 'seq')
- grad_dilated: float32 [1536, 3, 768], P(('groups', 'seq'))
- grad_project: float32 [1536, 768], P(('groups', 'seq'))
- grad_outer_gain: float32 [1536], P(('groups', 'seq'))
- grad_inner_gain: float32 [768], P(('groups', 'seq'))
All inputs are finite; a program needn't handle non-finite values.
Results may differ from a plain program's by a relative error of at most 0.0056.
Values may be sent and summed in bfloat16 or wider, within the bound.
No kernel may reach another device: no remote copies, remote signals or barrier semaphores. Data moves between devices by JAX's collectives and lax.ppermute only.
A program may use at most 128 MiB of HBM per device.

v0:
```python
import math
import jax
import jax.numpy as jnp
from jax import lax
from jax.sharding import PartitionSpec as P

KERNEL_TAPS = 3
DILATION_STEP = 32
eps = 1e-06


def padded(block, sides, width):
    for axis, dim in sides:
        count = lax.axis_size(axis)
        forward = [(i, i + 1) for i in range(count - 1)]
        backward = [(target, source) for source, target in forward]
        low = lax.ppermute(
            lax.slice_in_dim(block, block.shape[dim] - width, None, axis=dim), axis, forward
        )
        high = lax.ppermute(lax.slice_in_dim(block, 0, width, axis=dim), axis, backward)
        block = jnp.concatenate([low, block, high], axis=dim)
    return block


def act_norm(values, gain):
    meansq = jnp.mean(values * values, axis=-1, keepdims=True)
    return jax.nn.gelu(values * lax.rsqrt(meansq + eps) * gain, approximate=True)


def reduce_dilated(padded_input, conv_output_gradient, factor):
    bin_count = conv_output_gradient.shape[1]
    tap_slices = [
        jnp.einsum(
            "btc,bti->ci",
            padded_input[:, tap_index * DILATION_STEP : tap_index * DILATION_STEP + bin_count],
            conv_output_gradient,
            preferred_element_type=jnp.float32,
        )
        for tap_index in range(KERNEL_TAPS)
    ]
    return lax.psum_scatter(
        jnp.stack(tap_slices, axis=1) * factor, "seq", scatter_dimension=0, tiled=True
    )


def body(features, cotangent, dilated_kernel_weight, project_weight, outer_gain, inner_gain):
    bin_count = features.shape[1]
    factor = 1.0 / math.sqrt(features.shape[0] * bin_count * lax.axis_size("seq"))
    full_dilated = lax.all_gather(dilated_kernel_weight, "seq", axis=0, tiled=True)
    full_project = lax.all_gather(project_weight, "seq", axis=0, tiled=True)
    as_float = features.astype(jnp.float32)
    active_features = act_norm(as_float, outer_gain).astype(jnp.bfloat16)
    padded_input = padded(active_features, (("seq", 1),), DILATION_STEP)
    conv_output = jnp.einsum(
        "btc,ci->bti",
        padded_input[:, 0:bin_count],
        full_dilated[:, 0, :],
        preferred_element_type=jnp.float32,
    )
    for tap_index in range(1, KERNEL_TAPS):
        conv_output = conv_output + jnp.einsum(
            "btc,ci->bti",
            padded_input[:, tap_index * DILATION_STEP : tap_index * DILATION_STEP + bin_count],
            full_dilated[:, tap_index, :],
            preferred_element_type=jnp.float32,
        )
    hidden = act_norm(conv_output, inner_gain).astype(jnp.bfloat16)
    block_out = (
        as_float
        + jnp.einsum("bti,ci->btc", hidden, full_project, preferred_element_type=jnp.float32)
    ).astype(jnp.bfloat16)
    grad_hidden = jnp.einsum(
        "btc,ci->bti", cotangent, full_project, preferred_element_type=jnp.float32
    )
    unused, pull_inner = jax.vjp(act_norm, conv_output, inner_gain)
    conv_output_gradient, grad_gain_inner = pull_inner(grad_hidden)
    conv_output_gradient = conv_output_gradient.astype(jnp.bfloat16)
    padded_input_gradient = padded(conv_output_gradient, (("seq", 1),), DILATION_STEP)
    grad_active = jnp.zeros(features.shape, jnp.float32)
    for tap_index in range(KERNEL_TAPS):
        tap_shift = (KERNEL_TAPS - 1 - tap_index) * DILATION_STEP
        grad_active = grad_active + jnp.einsum(
            "bti,ci->btc",
            padded_input_gradient[:, tap_shift : tap_shift + bin_count],
            full_dilated[:, tap_index, :],
            preferred_element_type=jnp.float32,
        )
    unused_two, pull_outer = jax.vjp(act_norm, as_float, outer_gain)
    grad_branch, grad_gain_outer = pull_outer(grad_active)
    grad_features = (cotangent.astype(jnp.float32) + grad_branch).astype(jnp.bfloat16)
    grad_dilated = reduce_dilated(padded_input, conv_output_gradient, factor)
    grad_project = lax.psum_scatter(
        jnp.einsum("btc,bti->ci", cotangent, hidden, preferred_element_type=jnp.float32) * factor,
        "seq",
        scatter_dimension=0,
        tiled=True,
    )
    grad_outer_gain, grad_inner_gain = (
        lax.psum_scatter(grad_gain_outer * factor, "seq", scatter_dimension=0, tiled=True),
        lax.psum_scatter(grad_gain_inner * factor, "seq", scatter_dimension=0, tiled=True),
    )
    return (block_out, grad_features, grad_dilated, grad_project, grad_outer_gain, grad_inner_gain)


def solution(mesh):
    return jax.shard_map(
        body,
        mesh=mesh,
        in_specs=(
            P("groups", "seq", None),
            P("groups", "seq", None),
            P("seq", None, None),
            P("seq", None),
            P(),
            P(),
        ),
        out_specs=(
            P("groups", "seq", None),
            P("groups", "seq", None),
            P(("groups", "seq"), None, None),
            P(("groups", "seq"), None),
            P(("groups", "seq")),
            P(("groups", "seq")),
        ),
        check_vma=False,
    )
```

profile of v0, /device:TPU:0, one launch (start us, length us, event | category | flops | bytes accessed | tf_op | source)
XLA Modules:
  0.0 433.5 jit_solution(2068119754786179202)
XLA Ops:
  7.2 0.0 all-gather.3.cloned.1.call-start
  7.2 0.7 all-gather.3.cloned.1.call-update
  7.9 0.0 all-gather.5.cloned.1.call-start
  8.0 0.7 all-gather.5.cloned.1.call-update
  8.7 0.0 reduce-scatter.7.cloned.1.call-start
  8.7 1.4 fusion.27
  10.1 1.4 fusion.18
  11.5 2.4 collective-permute-start
  13.9 1.3 collective-permute-start.1
  15.2 71.3 %all-gather.3.cloned.1.call-done = bf16[1536,3,768]{2,0,1:T(8,128)(2,1)} async-done(((bf16[48,3,768]{2,0,1:T(8,128)(2,1)}), bf16[1536,3,768]{2,0,1:T(8,128)(2,1)}) %all-gather.3.cloned.1.call-update) | async-done | bytes 7077904 | tf_op jit(solution)/shard_map/all_gather | solution.py:49
  86.5 2.4 fusion.8
  89.0 0.0 collective-permute-done.1
  89.0 0.0 copy-start.4
  89.0 2.5 fusion.10
  91.5 0.0 copy-start.1
  91.5 0.0 copy-start.6
  91.5 0.0 collective-permute-done
  91.5 0.0 copy-start.2
  91.6 2.6 multiply_reduce_fusion.2
  94.2 3.2 fusion
  97.4 6.1 %copy.26 = f32[1536,768]{1,0:T(8,128)} copy(f32[1536,768]{0,1:T(8,128)} %fusion) | data formatting | bytes 9437184
  103.5 0.0 reduce-scatter.7.cloned.1.call-update
  103.5 0.0 reduce-scatter.5.cloned.1.call-start
  103.6 41.6 %all-gather.5.cloned.1.call-done = bf16[1536,768]{1,0:T(8,128)(2,1)} async-done(((bf16[48,768]{1,0:T(8,128)(2,1)}), bf16[1536,768]{1,0:T(8,128)(2,1)}) %all-gather.5.cloned.1.call-update) | async-done | bytes 2359312 | tf_op jit(solution)/shard_map/all_gather | solution.py:50
  145.2 3.6 multiply_reduce_fusion
  148.9 0.2 fusion.37
  149.1 0.7 copy-done.3
  149.8 0.8 convolution_bitcast_fusion.2
  150.6 0.1 copy-done.5
  150.7 0.8 convolution_bitcast_fusion
  151.5 0.8 convolution_bitcast_fusion.1
  152.4 5.5 %maximum_multiply_fusion = f32[1536,3,768]{2,0,1:T(8,128)} fusion(f32[1536,1,768]{2,0,1:T(8,128)S(1)} %convolution_bitcast_fusion, f32[1536,1,768]{2,0,1:T(8,128)S(1)} %convolution_bitcast_fusion.1, f32[1536,1,768]{2,0,1:T(8,128)S(1)} %convolution_bitcast_fusion.2), kind=kLoop, calls=%fused_computation | loop fusion | flops 10616832 | bytes 28311552 | tf_op jit(solution)/shard_map/mul | solution.py:42
  157.8 0.0 reduce-scatter.5.cloned.1.call-update
  157.9 2.3 collective-permute-start.3
  160.2 2.5 fusion.7
  162.8 1.9 fusion.2
  164.6 1.6 collective-permute-start.2
  166.3 0.0 collective-permute-done.3
  166.3 2.5 fusion.9
  168.8 0.0 collective-permute-done.2
  168.9 4.4 %fusion.21 = (f32[1536]{0:T(1024)S(1)}, f32[2,128]{1,0:T(2,128)}, f32[2,128,1536]{2,1,0:T(8,128)S(1)}) fusion(bf16[2,128,1536]{2,1,0:T(8,128)(2,1)S(1)} %copy-done, f32[2,128]{1,0:T(2,128)S(1)} %copy-done.9, f32[1536]{0:T(1024)S(1)} %copy-done.7, f32[2,128,1536]{2,1,0:T(8,128)S(1)} %fusion.9, f32[2,128,1536]{2,1,0:T(8,128)S(1)} %fusion.7, ...), kind=kOutput, calls=%fused_computation.38 | convolution fusion | flops 616167680 | bytes 8370176 | tf_op jit(solution)/shard_map/bti,ci->btc/dot_general | solution.py:82
  173.3 42.5 %all-reduce.2 = (f32[1536]{0:T(1024)S(1)}, f32[768]{0:T(1024)S(1)}) all-reduce(f32[1536]{0:T(1024)S(1)} %broadcast_multiply_fusion, f32[768]{0:T(1024)S(1)} %broadcast_multiply_fusion.1), channel_id=4, replica_groups=mesh['groups'=1,'seq'=32] {'seq'}, use_global_device_ids=true, to_apply=%region_7.0.clone | all-reduce | flops 2304 | bytes 18432
  215.8 0.6 dynamic-slice
  216.4 0.6 dynamic-slice.1
  217.0 0.7 multiply_multiply_fusion.5
  217.7 2.1 fusion.26
  219.8 37.8 %reduce-scatter.7.cloned.1.call-done = f32[48,768]{1,0:T(8,128)} async-done(((f32[1536,768]{1,0:T(8,128)}), f32[48,768]{1,0:T(8,128)}) %reduce-scatter.7.cloned.1.call-update) | async-done | bytes 147472
  257.5 169.5 %reduce-scatter.5.cloned.1.call-done = f32[48,3,768]{2,0,1:T(8,128)} async-done(((f32[1536,3,768]{2,0,1:T(8,128)}), f32[48,3,768]{2,0,1:T(8,128)}) %reduce-scatter.5.cloned.1.call-update) | async-done | bytes 442384 | tf_op jit(solution)/shard_map/reduce_scatter | solution.py:41
  (25 shorter events, 0.1 us)
Async XLA Ops:
  7.2 2.9 copy-start
  7.2 79.3 %all-gather.3.cloned.1.call-start = ((), (), s32[]{:S(2)}) async-start(), calls=%async_computation.2 | async-start | bytes 7299072 | tf_op jit(solution)/shard_map/all_gather | solution.py:49
  7.9 137.3 %all-gather.5.cloned.1.call-start = ((), (), s32[]{:S(2)}) async-start(), calls=%async_computation.3 | async-start | bytes 2433024 | tf_op jit(solution)/shard_map/all_gather | solution.py:50
  8.7 248.9 %reduce-scatter.7.cloned.1.call-start = ((), (), s32[]{:S(2)}) async-start(), calls=%async_computation.5 | async-start | bytes 4866048
  10.1 78.9 %copy-start.8 = (f32[2,128]{1,0:T(2,128)}, f32[2,128]{1,0:T(2,128)S(1)}, u32[]{:S(2)}) copy-start(f32[2,128]{1,0:T(2,128)S(1)} %fusion.42) | copy-start | bytes 3076
  11.5 80.0 %collective-permute-start = (bf16[2,32,1536]{2,1,0:T(8,128)(2,1)S(1)}, bf16[2,32,1536]{2,1,0:T(8,128)(2,1)S(1)}, u32[]{:S(2)}, u32[]{:S(2)}) collective-permute-start(bf16[2,32,1536]{2,1,0:T(8,128)(2,1)S(1)} %get-tuple-element.24), channel_id=1, source_target_pairs={{0,1},{1,2},{2,3},{3,4},{4,5},{5,6},{6,7},{7,8},{8,9},{9,10},{10,1... | collective-permute-start | bytes 589832 | tf_op jit(solution)/shard_map/ppermute | solution.py:17
  13.9 75.0 %collective-permute-start.1 = (bf16[2,32,1536]{2,1,0:T(8,128)(2,1)S(1)}, bf16[2,32,1536]{2,1,0:T(8,128)(2,1)S(1)}, u32[]{:S(2)}, u32[]{:S(2)}) collective-permute-start(bf16[2,32,1536]{2,1,0:T(8,128)(2,1)S(1)} %get-tuple-element.25), channel_id=1, source_target_pairs={{1,0},{2,1},{3,2},{4,3},{5,4},{6,5},{7,6},{8,7},{9,8},{10,9},{11,1... | collective-permute-start | bytes 589832 | tf_op jit(solution)/shard_map/ppermute | solution.py:20
  89.0 2.5 copy-start.4
  91.5 2.7 copy-start.1
  91.5 2.7 copy-start.6
  91.5 2.7 copy-start.2
  103.5 323.5 %reduce-scatter.5.cloned.1.call-start = ((), (), s32[]{:S(2)}) async-start(), calls=%async_computation.4 | async-start | bytes 14598144 | tf_op jit(solution)/shard_map/reduce_scatter | solution.py:41
  148.8 0.9 copy-start.3
  149.8 0.9 copy-start.5
  157.9 4.9 %copy-start.11 = (bf16[1536,768]{1,0:T(8,128)(2,1)S(1)}, bf16[1536,768]{1,0:T(8,128)(2,1)}, u32[]{:S(2)}) copy-start(bf16[1536,768]{1,0:T(8,128)(2,1)} %all-gather.5.cloned.1.call-done) | copy-start | bytes 7077892
  157.9 8.4 %collective-permute-start.3 = (bf16[2,32,768]{2,1,0:T(8,128)(2,1)S(1)}, bf16[2,32,768]{2,1,0:T(8,128)(2,1)S(1)}, u32[]{:S(2)}, u32[]{:S(2)}) collective-permute-start(bf16[2,32,768]{2,1,0:T(8,128)(2,1)S(1)} %get-tuple-element.27), channel_id=1, source_target_pairs={{0,1},{1,2},{2,3},{3,4},{4,5},{5,6},{6,7},{7,8},{8,9},{9,10},{10,1... | collective-permute-start | bytes 294920 | tf_op jit(solution)/shard_map/ppermute | solution.py:17
  162.8 1.9 copy-start.10
  164.6 4.2 copy-start.7
  164.6 4.2 copy-start.9
  164.6 4.2 collective-permute-start.2
Sparse Core Ops, SparseCore 0:
  11.0 75.5 all-gather.2
  89.4 55.7 all-gather.4
  151.3 106.2 reduce-scatter.6
  265.0 161.9 reduce-scatter.4
where the time goes:
time: 434 us
  waiting for transfers between devices  322 us (74%)
  blocking collectives  42.5 us (10%)
  matrix products  28.2 us (6%)
  between operations  14.1 us (3%)
  other arithmetic  11.2 us (3%)
  local copies, waits for them, and re-layouts  8.18 us (2%)
  starting transfers between devices  7.73 us (2%)
    reduce_scatter x1, waiting for transfers between devices, reduce_dilated(): lax.psum_scatter(jnp.stack(tap_slices, axis=1) * factor, 'seq', scatter_d...  169 us
    all_gather x1, waiting for transfers between devices, body(): lax.all_gather(dilated_kernel_weight, 'seq', axis=0, tiled=True)  71.3 us
    unnamed x1, blocking collectives  42.5 us
    all_gather x1, waiting for transfers between devices, body(): full_project = lax.all_gather(project_weight, 'seq', axis=0, tiled=True)  41.6 us
    unnamed x5, waiting for transfers between devices  39.2 us
    dot_general x3, matrix products, body(): jnp.einsum('bti,ci->btc', padded_input_gradient[:, tap_shift:tap_shift +...  9.53 us
  transfers between devices with their start and end apart: 8, of which 4 were waited for; matrix products, arithmetic and copies ran while one was open for 11% of the time, Pallas kernels for 0%

commit v1 on v0

--- a/solution.py
+++ b/solution.py
@@ -47,7 +47,14 @@
     bin_count = features.shape[1]
     factor = 1.0 / math.sqrt(features.shape[0] * bin_count * lax.axis_size("seq"))
     full_dilated = lax.all_gather(dilated_kernel_weight, "seq", axis=0, tiled=True)
-    full_project = lax.all_gather(project_weight, "seq", axis=0, tiled=True)
+    ways, here, step = (lax.axis_size("seq"), lax.axis_index("seq"), project_weight.shape[0])
+    line, have = (project_weight, 1)
+    while have < ways:
+        line = jnp.concatenate(
+            [line, lax.ppermute(line, "seq", [(d, (d - have) % ways) for d in range(ways)])], axis=0
+        )
+        have = 2 * have
+    full_project = jnp.roll(line, here * step, axis=0)
     as_float = features.astype(jnp.float32)
     active_features = act_norm(as_float, outer_gain).astype(jnp.bfloat16)
     padded_input = padded(active_features, (("seq", 1),), DILATION_STEP)

time: 434 us -> 403 us (0.929)
  waiting for transfers between devices: 322 us -> 264 us
  starting transfers between devices: 7.73 us -> 20.6 us
  local copies, waits for them, and re-layouts: 8.18 us -> 18.9 us
    ppermute x0 -> x5, waiting for transfers between devices: none -> 87.2 us  [body(): lax.ppermute(line, 'seq', [(d, (d - have) % ways) for d in range(ways)])]
    reduce_scatter x1, waiting for transfers between devices: 169 us -> 106 us  [reduce_dilated(): lax.psum_scatter(jnp.stack(tap_slices, axis=1) * factor, 'seq', scatter_d...]
    all_gather x1 -> x0, waiting for transfers between devices: 41.6 us -> none  [body(): full_project = lax.all_gather(project_weight, 'seq', axis=0, tiled=True)]
    unnamed x5 -> x4, waiting for transfers between devices: 39.2 us -> 0.72 us
    ppermute x0 -> x5, starting transfers between devices: none -> 15 us  [body(): lax.ppermute(line, 'seq', [(d, (d - have) % ways) for d in range(ways)])]
    unnamed x27 -> x43, local copies, waits for them, and re-layouts: 8.13 us -> 16.6 us
    all_gather x1, waiting for transfers between devices: 71.3 us -> 66.3 us  [body(): lax.all_gather(dilated_kernel_weight, 'seq', axis=0, tiled=True)]
    ppermute x2, waiting for transfers between devices: 0.01 us -> 4.46 us  [padded(): lax.ppermute(lax.slice_in_dim(block, 0, width, axis=dim), axis, backward)]
  transfers between devices with their start and end apart: 8 -> 12, of which waited for: 4 -> 7; matrix products, arithmetic and copies ran while one was open for 11% -> 15% of each run, Pallas kernels for 0% -> 0%
where the time goes in v1:
time: 403 us; the launch traced here: 402 us
  waiting for transfers between devices  264 us (66%)
  blocking collectives  42.8 us (11%)
  matrix products  29.6 us (7%)
  starting transfers between devices  20.6 us (5%)
  local copies, waits for them, and re-layouts  18.9 us (5%)
  between operations  14.1 us (3%)
  other arithmetic  11.7 us (3%)
    reduce_scatter x1, waiting for transfers between devices, reduce_dilated(): lax.psum_scatter(jnp.stack(tap_slices, axis=1) * factor, 'seq', scatter_d...  106 us
    ppermute x5, waiting for transfers between devices, body(): lax.ppermute(line, 'seq', [(d, (d - have) % ways) for d in range(ways)])  87.2 us
    all_gather x1, waiting for transfers between devices, body(): lax.all_gather(dilated_kernel_weight, 'seq', axis=0, tiled=True)  66.3 us
    unnamed x1, blocking collectives  42.8 us
    unnamed x43, local copies, waits for them, and re-layouts  16.6 us
    ppermute x5, starting transfers between devices, body(): lax.ppermute(line, 'seq', [(d, (d - have) % ways) for d in range(ways)])  15 us
    dot_general x3, matrix products, body(): jnp.einsum('bti,ci->btc', padded_input_gradient[:, tap_shift:tap_shift +...  9.47 us
  transfers between devices with their start and end apart: 12, of which 7 were waited for; matrix products, arithmetic and copies ran while one was open for 15% of the time, Pallas kernels for 0%

profile of v1, /device:TPU:0, one launch (start us, length us, event | category | flops | bytes accessed | tf_op | source)
XLA Modules:
  0.0 401.9 jit_solution(3701750761538321572)
XLA Ops:
  7.2 0.7 all-gather.2.cloned.1.call-update
  7.9 6.4 %collective-permute-start.2 = (bf16[48,768]{1,0:T(8,128)(2,1)}, bf16[48,768]{1,0:T(8,128)(2,1)S(1)}, u32[]{:S(2)}, u32[]{:S(2)}) collective-permute-start(bf16[48,768]{1,0:T(8,128)(2,1)} %param.9), channel_id=1, source_target_pairs={{0,31},{1,0},{2,1},{3,2},{4,3},{5,4},{6,5},{7,6},{8,7},{9,8},{10,9... | collective-permute-start | bytes 221192 | tf_op jit(solution)/shard_map/ppermute | solution.py:54
  14.4 1.4 fusion.29
  15.8 1.8 fusion.20
  17.6 1.3 collective-permute-start
  19.0 1.3 collective-permute-start.1
  20.3 66.3 %all-gather.2.cloned.1.call-done = bf16[1536,3,768]{2,0,1:T(8,128)(2,1)} async-done(((bf16[48,3,768]{2,0,1:T(8,128)(2,1)}), bf16[1536,3,768]{2,0,1:T(8,128)(2,1)}) %all-gather.2.cloned.1.call-update) | async-done | bytes 7077904 | tf_op jit(solution)/shard_map/all_gather | solution.py:49
  86.5 2.4 fusion.8
  89.0 2.5 fusion.10
  91.6 2.6 multiply_reduce_fusion.2
  94.2 3.1 fusion
  97.4 6.1 %copy.26 = f32[1536,768]{1,0:T(8,128)} copy(f32[1536,768]{0,1:T(8,128)} %fusion) | data formatting | bytes 9437184
  103.6 0.8 copy-done.6
  104.4 2.8 collective-permute-start.3
  107.2 3.5 collective-permute-done.3
  110.8 2.5 collective-permute-start.4
  113.3 5.9 %collective-permute-done.4 = bf16[192,768]{1,0:T(8,128)(2,1)S(1)} collective-permute-done((bf16[192,768]{1,0:T(8,128)(2,1)S(1)}, bf16[192,768]{1,0:T(8,128)(2,1)S(1)}, u32[]{:S(2)}, u32[]{:S(2)}) %collective-permute-start.4) | collective-permute-done | bytes 294944 | tf_op jit(solution)/shard_map/ppermute | solution.py:54
  119.2 1.6 collective-permute-start.5
  120.9 0.7 constant_dynamic-update-slice_fusion.4
  121.5 0.7 constant_dynamic-update-slice_fusion.3
  122.2 0.7 constant_dynamic-update-slice_fusion.2
  122.9 0.9 constant_dynamic-update-slice_fusion.1
  123.8 9.2 %collective-permute-done.5 = bf16[384,768]{1,0:T(8,128)(2,1)S(1)} collective-permute-done((bf16[384,768]{1,0:T(8,128)(2,1)S(1)}, bf16[384,768]{1,0:T(8,128)(2,1)S(1)}, u32[]{:S(2)}, u32[]{:S(2)}) %collective-permute-start.5) | collective-permute-done | bytes 589856 | tf_op jit(solution)/shard_map/ppermute | solution.py:54
  133.0 1.2 constant_dynamic-update-slice_fusion
  134.2 1.6 collective-permute-start.6
  135.8 68.5 %collective-permute-done.6 = bf16[768,768]{1,0:T(8,128)(2,1)S(1)} collective-permute-done((bf16[768,768]{1,0:T(8,128)(2,1)}, bf16[768,768]{1,0:T(8,128)(2,1)S(1)}, u32[]{:S(2)}, u32[]{:S(2)}) %collective-permute-start.6) | collective-permute-done | bytes 1179680 | tf_op jit(solution)/shard_map/ppermute | solution.py:54
  204.3 1.1 constant_dynamic-update-slice_fusion.11
  206.7 0.7 constant_dynamic-update-slice_fusion.8
  207.4 0.7 constant_dynamic-update-slice_fusion.7
  208.1 0.9 constant_dynamic-update-slice_fusion.6
  209.0 1.1 constant_dynamic-update-slice_fusion.5
  210.1 3.1 multiply_reduce_fusion
  213.5 0.7 copy-done.8
  214.2 0.8 convolution_bitcast_fusion.2
  215.1 0.8 convolution_bitcast_fusion
  215.9 0.8 convolution_bitcast_fusion.1
  216.8 5.4 %maximum_multiply_fusion = f32[1536,3,768]{2,0,1:T(8,128)} fusion(f32[1536,1,768]{2,0,1:T(8,128)S(1)} %convolution_bitcast_fusion, f32[1536,1,768]{2,0,1:T(8,128)S(1)} %convolution_bitcast_fusion.1, f32[1536,1,768]{2,0,1:T(8,128)S(1)} %convolution_bitcast_fusion.2), kind=kLoop, calls=%fused_computation | loop fusion | flops 10616832 | bytes 28311552 | tf_op jit(solution)/shard_map/mul | solution.py:42
  222.3 1.4 collective-permute-start.8
  223.7 3.8 fusion.2
  227.5 2.5 fusion.7
  230.0 1.5 collective-permute-start.7
  231.5 2.5 fusion.9
  234.0 4.5 %collective-permute-done.7 = bf16[2,32,768]{2,1,0:T(8,128)(2,1)S(1)} collective-permute-done((bf16[2,32,768]{2,1,0:T(8,128)(2,1)S(1)}, bf16[2,32,768]{2,1,0:T(8,128)(2,1)S(1)}, u32[]{:S(2)}, u32[]{:S(2)}) %collective-permute-start.7) | collective-permute-done | bytes 98336 | tf_op jit(solution)/shard_map/ppermute | solution.py:20
  238.5 4.5 %fusion.23 = (f32[1536]{0:T(1024)S(1)}, f32[2,128]{1,0:T(2,128)}, f32[2,128,1536]{2,1,0:T(8,128)S(1)}) fusion(bf16[2,128,1536]{2,1,0:T(8,128)(2,1)S(1)} %copy-done, f32[2,128]{1,0:T(2,128)S(1)} %copy-done.14, f32[1536]{0:T(1024)S(1)} %copy-done.12, f32[2,128,1536]{2,1,0:T(8,128)S(1)} %fusion.9, f32[2,128,1536]{2,1,0:T(8,128)S(1)} %fusion.7, ...), kind=kOutput, calls=%fused_computation.40 | convolution fusion | flops 616167680 | bytes 8370176 | tf_op jit(solution)/shard_map/bti,ci->btc/dot_general | solution.py:89
  243.0 42.8 %all-reduce.2 = (f32[1536]{0:T(1024)S(1)}, f32[768]{0:T(1024)S(1)}) all-reduce(f32[1536]{0:T(1024)S(1)} %broadcast_multiply_fusion, f32[768]{0:T(1024)S(1)} %broadcast_multiply_fusion.1), channel_id=4, replica_groups=mesh['groups'=1,'seq'=32] {'seq'}, use_global_device_ids=true, to_apply=%region_7.8.clone | all-reduce | flops 2304 | bytes 18432
  287.0 0.7 multiply_multiply_fusion.5
  287.7 2.1 fusion.28
  289.7 105.7 %reduce-scatter.5.cloned.1.call-done = f32[48,3,768]{2,0,1:T(8,128)} async-done(((f32[1536,3,768]{2,0,1:T(8,128)}), f32[48,3,768]{2,0,1:T(8,128)}) %reduce-scatter.5.cloned.1.call-update) | async-done | bytes 442384 | tf_op jit(solution)/shard_map/reduce_scatter | solution.py:41
  (53 shorter events, 3.1 us)
Async XLA Ops:
  7.2 79.3 %all-gather.2.cloned.1.call-start = ((), (), s32[]{:S(2)}) async-start(), calls=%async_computation.2 | async-start | bytes 7299072 | tf_op jit(solution)/shard_map/all_gather | solution.py:49
  7.9 281.8 %reduce-scatter.7.cloned.1.call-start = ((), (), s32[]{:S(2)}) async-start(), calls=%async_computation.4 | async-start | bytes 4866048
  7.9 95.6 %collective-permute-start.2 = (bf16[48,768]{1,0:T(8,128)(2,1)}, bf16[48,768]{1,0:T(8,128)(2,1)S(1)}, u32[]{:S(2)}, u32[]{:S(2)}) collective-permute-start(bf16[48,768]{1,0:T(8,128)(2,1)} %param.9), channel_id=1, source_target_pairs={{0,31},{1,0},{2,1},{3,2},{4,3},{5,4},{6,5},{7,6},{8,7},{9,8},{10,9... | collective-permute-start | bytes 221192 | tf_op jit(solution)/shard_map/ppermute | solution.py:54
  15.7 73.2 %copy-start.13 = (f32[2,128]{1,0:T(2,128)}, f32[2,128]{1,0:T(2,128)S(1)}, u32[]{:S(2)}) copy-start(f32[2,128]{1,0:T(2,128)S(1)} %fusion.47) | copy-start | bytes 3076
  17.6 73.9 %collective-permute-start = (bf16[2,32,1536]{2,1,0:T(8,128)(2,1)S(1)}, bf16[2,32,1536]{2,1,0:T(8,128)(2,1)S(1)}, u32[]{:S(2)}, u32[]{:S(2)}) collective-permute-start(bf16[2,32,1536]{2,1,0:T(8,128)(2,1)S(1)} %get-tuple-element.24), channel_id=1, source_target_pairs={{0,1},{1,2},{2,3},{3,4},{4,5},{5,6},{6,7},{7,8},{8,9},{9,10},{10,1... | collective-permute-start | bytes 589832 | tf_op jit(solution)/shard_map/ppermute | solution.py:17
  19.0 70.0 %collective-permute-start.1 = (bf16[2,32,1536]{2,1,0:T(8,128)(2,1)S(1)}, bf16[2,32,1536]{2,1,0:T(8,128)(2,1)S(1)}, u32[]{:S(2)}, u32[]{:S(2)}) collective-permute-start(bf16[2,32,1536]{2,1,0:T(8,128)(2,1)S(1)} %get-tuple-element.25), channel_id=1, source_target_pairs={{1,0},{2,1},{3,2},{4,3},{5,4},{6,5},{7,6},{8,7},{9,8},{10,9},{11,1... | collective-permute-start | bytes 589832 | tf_op jit(solution)/shard_map/ppermute | solution.py:20
  89.0 2.5 copy-start.9
  91.5 2.7 copy-start.1
  91.5 2.7 copy-start.11
  91.5 2.7 copy-start.7
  103.5 0.9 copy-start.6
  103.5 291.8 %reduce-scatter.5.cloned.1.call-start = ((), (), s32[]{:S(2)}) async-start(), calls=%async_computation.3 | async-start | bytes 14598144 | tf_op jit(solution)/shard_map/reduce_scatter | solution.py:41
  104.4 6.3 %collective-permute-start.3 = (bf16[96,768]{1,0:T(8,128)(2,1)S(1)}, bf16[96,768]{1,0:T(8,128)(2,1)S(1)}, u32[]{:S(2)}, u32[]{:S(2)}) collective-permute-start(bf16[96,768]{1,0:T(8,128)(2,1)S(1)} %pad_maximum_fusion.12), channel_id=1, source_target_pairs={{0,30},{1,31},{2,0},{3,1},{4,2},{5,3},{6,4},{7,5},{8,6},{9,7},{10,... | collective-permute-start | bytes 442376 | tf_op jit(solution)/shard_map/ppermute | solution.py:54
  110.8 8.4 %collective-permute-start.4 = (bf16[192,768]{1,0:T(8,128)(2,1)S(1)}, bf16[192,768]{1,0:T(8,128)(2,1)S(1)}, u32[]{:S(2)}, u32[]{:S(2)}) collective-permute-start(bf16[192,768]{1,0:T(8,128)(2,1)S(1)} %pad_maximum_fusion.11), channel_id=1, source_target_pairs={{0,28},{1,29},{2,30},{3,31},{4,0},{5,1},{6,2},{7,3},{8,4},{9,5},{1... | collective-permute-start | bytes 884744 | tf_op jit(solution)/shard_map/ppermute | solution.py:54
  119.2 13.8 %collective-permute-start.5 = (bf16[384,768]{1,0:T(8,128)(2,1)S(1)}, bf16[384,768]{1,0:T(8,128)(2,1)S(1)}, u32[]{:S(2)}, u32[]{:S(2)}) collective-permute-start(bf16[384,768]{1,0:T(8,128)(2,1)S(1)} %pad_maximum_fusion.2), channel_id=1, source_target_pairs={{0,24},{1,25},{2,26},{3,27},{4,28},{5,29},{6,30},{7,31},{8,0},{9,1... | collective-permute-start | bytes 1769480 | tf_op jit(solution)/shard_map/ppermute | solution.py:54
  133.0 1.2 copy-start.4
  134.2 70.1 %collective-permute-start.6 = (bf16[768,768]{1,0:T(8,128)(2,1)}, bf16[768,768]{1,0:T(8,128)(2,1)S(1)}, u32[]{:S(2)}, u32[]{:S(2)}) collective-permute-start(bf16[768,768]{1,0:T(8,128)(2,1)} %get-tuple-element.26), channel_id=1, source_target_pairs={{0,16},{1,17},{2,18},{3,19},{4,20},{5,21},{6,22},{7,23},{8,24},{9,... | collective-permute-start | bytes 3538952 | tf_op jit(solution)/shard_map/ppermute | solution.py:54
  204.3 3.8 copy-start.5
  208.1 2.0 copy-start.2
  213.3 0.9 copy-start.8
  214.2 0.9 copy-start.10
  222.2 1.5 copy-start
  222.3 9.2 %collective-permute-start.8 = (bf16[2,32,768]{2,1,0:T(8,128)(2,1)S(1)}, bf16[2,32,768]{2,1,0:T(8,128)(2,1)S(1)}, u32[]{:S(2)}, u32[]{:S(2)}) collective-permute-start(bf16[2,32,768]{2,1,0:T(8,128)(2,1)S(1)} %get-tuple-element.29), channel_id=1, source_target_pairs={{0,1},{1,2},{2,3},{3,4},{4,5},{5,6},{6,7},{7,8},{8,9},{9,10},{10,1... | collective-permute-start | bytes 294920 | tf_op jit(solution)/shard_map/ppermute | solution.py:17
  230.0 8.5 %copy-start.12 = (f32[1536]{0:T(1024)S(1)}, f32[1536]{0:T(1024)}, u32[]{:S(2)}) copy-start(f32[1536]{0:T(1024)} %param.10) | copy-start | bytes 18436
  230.0 8.5 %copy-start.14 = (f32[2,128]{1,0:T(2,128)S(1)}, f32[2,128]{1,0:T(2,128)}, u32[]{:S(2)}) copy-start(f32[2,128]{1,0:T(2,128)} %copy-done.13) | copy-start | bytes 3076
  230.0 8.4 %collective-permute-start.7 = (bf16[2,32,768]{2,1,0:T(8,128)(2,1)S(1)}, bf16[2,32,768]{2,1,0:T(8,128)(2,1)S(1)}, u32[]{:S(2)}, u32[]{:S(2)}) collective-permute-start(bf16[2,32,768]{2,1,0:T(8,128)(2,1)S(1)} %get-tuple-element.28), channel_id=1, source_target_pairs={{1,0},{2,1},{3,2},{4,3},{5,4},{6,5},{7,6},{8,7},{9,8},{10,9},{11,1... | collective-permute-start | bytes 294920 | tf_op jit(solution)/shard_map/ppermute | solution.py:20
  234.0 53.6 %copy-start.3 = (bf16[2,128,1536]{2,1,0:T(8,128)(2,1)S(1)}, bf16[2,128,1536]{2,1,0:T(8,128)(2,1)}, u32[]{:S(2)}) copy-start(bf16[2,128,1536]{2,1,0:T(8,128)(2,1)} %param.7) | copy-start | bytes 2359300
Sparse Core Ops, SparseCore 0:
  10.9 75.5 all-gather.1
  103.6 122.0 reduce-scatter.6
  233.3 161.9 reduce-scatter.4
